TPU v7x, 32 devices: a whole 2x2x4 slice. The times are simulated.
32 devices in a mesh: area: 8 (over z, x), tile: 4 (over y, core).
Axes of the slice: x: 2, y: 2, z: 4, core: 2. Of those that a mesh axis runs over, the one named last changes fastest.
Arguments:
- start_rates: bfloat16 [8, 256, 4096], P('area', None, 'tile'), may hold values from -0.8984375 to 0.8984375
- stim_drive: bfloat16 [8, 256, 4096], P('area', None, 'tile'), may hold values from -6 to 6
- leak_rates: float32 [8, 4096], P('area', 'tile'), may hold values from 0.2 to 0.9
- block_weights: bfloat16 [8, 32, 20, 128, 128], P('area', 'tile'), may hold values from -0.21875 to 0.21875
- near_index: int32 [8, 32, 12], P('area', 'tile'), may hold values from 0 to 9, as said below
- far_index: int32 [8, 32, 8], P('area', 'tile'), may hold values from 0 to 7, as said below
Outputs:
- final_rates: bfloat16 [8, 256, 4096], P('area', None, 'tile')
Inputs may be any that keep to these rules, and one draw needn't show every extreme that they name: `near_index`: an entry names one of the tile's own blocks (1 to 8) or the adjacent edge block of the neighbouring tile (0 the lower, 9 the upper). Slot 0 of every tile's first row block is 0 and slot 1 of every tile's last row block is 9. `far_index`: an entry q names the projecting block (the first block) of the same tile in section q, a section of another area; the areas are the consecutive groups of 3, 2, 2 and 1 eighths of the sections, in that order.
All inputs are finite; a program needn't handle non-finite values.
Results may differ from a plain program's by a relative error of at most 0.005.
Values may be sent and summed in bfloat16 or wider, within the bound.
A program may use at most 64 MiB of HBM per device.

v0:
```python
import functools

import jax
import jax.numpy as jnp
from jax import lax
from jax.experimental import pallas as pl
from jax.experimental.pallas import tpu as pltpu
from jax.sharding import PartitionSpec as P

STEPS = 3
CHUNKS = 2
LEAD = 1
UNROLL = 4
MESH = pl.DeviceIdType.MESH


def group_of(section, n_area):
    unit = n_area // 8
    return (
        (section >= 3 * unit).astype(jnp.int32)
        + (section >= 5 * unit).astype(jnp.int32)
        + (section >= 7 * unit).astype(jnp.int32)
    )


def kernel(sizes, near_idx, far_idx, rates_hbm, drive_hbm, leak_ref, w_hbm, out_ref, *scratch):
    n_area, n_tile, batch, rows, k_near, k_far, blk = sizes
    n_col = n_area // 2
    part = batch // CHUNKS
    nears = scratch[:STEPS]
    scratch = scratch[STEPS:]
    fars = [scratch[t * CHUNKS : (t + 1) * CHUNKS] for t in range(STEPS)]
    (
        drive, weights, acc,
        load_sem, drive_sem, w_sem,
        far_recv, col_send, own_send, relay_send, edge_send, edge_recv,
    ) = scratch[STEPS * CHUNKS :]

    area = lax.axis_index("area")
    tile = lax.axis_index("tile")
    side = lax.rem(area, 2)
    level = area // 2
    partner = area + 1 - 2 * side

    def needs(section, source):
        return group_of(section, n_area) != group_of(source, n_area)

    def column_needs(section, source):
        mate = section + 1 - 2 * lax.rem(section, 2)
        return jnp.logical_or(needs(section, source), needs(mate, source))

    def offsets(far_first):
        steps = range(n_col - 1, 0, -1) if far_first else range(1, n_col)
        return [s * d for d in steps for s in (1, -1)]

    def inside(offset):
        return jnp.logical_and(level + offset >= 0, level + offset < n_col)

    def member(offset):
        return area + 2 * offset

    def span(c):
        return pl.ds(c * part, part)

    def load(r):
        return pltpu.make_async_copy(
            rates_hbm.at[:, pl.ds(r * blk, blk)], nears[0].at[r + 1], load_sem.at[r]
        )

    def load_drive(r):
        return pltpu.make_async_copy(
            drive_hbm.at[:, pl.ds(r * blk, blk)], drive.at[r], drive_sem.at[r]
        )

    def load_weights(r):
        return pltpu.make_async_copy(w_hbm.at[r], weights.at[r], w_sem.at[r])

    order = [0, rows - 1] + list(range(1, rows - 1))
    for r in order:
        load(r).start()
    for r in range(rows):
        load_weights(r).start()
        load_drive(r).start()

    barrier = pltpu.get_barrier_semaphore()
    for offset in offsets(True):
        @pl.when(inside(offset))
        def _(offset=offset):
            pl.semaphore_signal(
                barrier, inc=1, device_id=(member(offset), tile), device_id_type=MESH
            )
    pl.semaphore_signal(barrier, inc=1, device_id=(partner, tile), device_id_type=MESH)
    has_low = tile > 0
    has_high = tile < n_tile - 1

    @pl.when(has_low)
    def _():
        pl.semaphore_signal(barrier, inc=1, device_id=(area, tile - 1), device_id_type=MESH)

    @pl.when(has_high)
    def _():
        pl.semaphore_signal(barrier, inc=1, device_id=(area, tile + 1), device_id_type=MESH)

    for t in range(STEPS):
        @pl.when(jnp.logical_not(has_low))
        def _(t=t):
            nears[t][0] = jnp.zeros((batch, blk), jnp.bfloat16)

        @pl.when(jnp.logical_not(has_high))
        def _(t=t):
            nears[t][rows + 1] = jnp.zeros((batch, blk), jnp.bfloat16)

    pl.semaphore_wait(
        barrier, n_col + has_low.astype(jnp.int32) + has_high.astype(jnp.int32)
    )

    def column_copy(t, c, offset):
        return pltpu.make_async_remote_copy(
            src_ref=nears[t].at[1, span(c)],
            dst_ref=fars[t][c].at[area],
            send_sem=col_send.at[t, c, offset + n_col - 1],
            recv_sem=far_recv.at[t, c, area],
            device_id=(member(offset), tile),
            device_id_type=MESH,
        )

    def own_copy(t, c):
        return pltpu.make_async_remote_copy(
            src_ref=nears[t].at[1, span(c)],
            dst_ref=fars[t][c].at[area],
            send_sem=own_send.at[t, c],
            recv_sem=far_recv.at[t, c, area],
            device_id=(partner, tile),
            device_id_type=MESH,
        )

    def relay_copy(t, c, offset):
        source = member(offset)
        return pltpu.make_async_remote_copy(
            src_ref=fars[t][c].at[source],
            dst_ref=fars[t][c].at[source],
            send_sem=relay_send.at[t, c, offset + n_col - 1],
            recv_sem=far_recv.at[t, c, source],
            device_id=(partner, tile),
            device_id_type=MESH,
        )

    def arrival(t, c, source):
        return pltpu.make_async_remote_copy(
            src_ref=nears[t].at[1, span(c)],
            dst_ref=fars[t][c].at[source],
            send_sem=own_send.at[t, c],
            recv_sem=far_recv.at[t, c, source],
            device_id=(partner, tile),
            device_id_type=MESH,
        )

    def low_copy(t):
        return pltpu.make_async_remote_copy(
            src_ref=nears[t].at[1],
            dst_ref=nears[t].at[rows + 1],
            send_sem=edge_send.at[t, 0],
            recv_sem=edge_recv.at[t, 1],
            device_id=(area, tile - 1),
            device_id_type=MESH,
        )

    def high_copy(t):
        return pltpu.make_async_remote_copy(
            src_ref=nears[t].at[rows],
            dst_ref=nears[t].at[0],
            send_sem=edge_send.at[t, 1],
            recv_sem=edge_recv.at[t, 0],
            device_id=(area, tile + 1),
            device_id_type=MESH,
        )

    def send_export(t, c):
        for offset in offsets(False):
            @pl.when(inside(offset))
            def _(offset=offset):
                @pl.when(column_needs(member(offset), area))
                def _():
                    column_copy(t, c, offset).start()

        @pl.when(needs(partner, area))
        def _():
            own_copy(t, c).start()

    def send_low(t):
        @pl.when(has_low)
        def _():
            low_copy(t).start()

    def send_high(t):
        @pl.when(has_high)
        def _():
            high_copy(t).start()

    def wait_edges(t):
        @pl.when(has_high)
        def _():
            low_copy(t).wait_recv()

        @pl.when(has_low)
        def _():
            high_copy(t).wait_recv()

    def relay(t, c):
        for offset in offsets(False):
            @pl.when(inside(offset))
            def _(offset=offset):
                @pl.when(column_needs(area, member(offset)))
                def _():
                    arrival(t, c, member(offset)).wait_recv()

                @pl.when(needs(partner, member(offset)))
                def _():
                    relay_copy(t, c, offset).start()

    def wait_partner(t, c):
        @pl.when(needs(area, partner))
        def _():
            arrival(t, c, partner).wait_recv()

        for offset in offsets(False):
            @pl.when(inside(offset))
            def _(offset=offset):
                source = partner + 2 * offset

                @pl.when(needs(area, source))
                def _():
                    arrival(t, c, source).wait_recv()

    def chain(pieces, w_of):
        total = None
        for k in range(0, len(pieces), 2):
            pair = jnp.concatenate([p() for p in pieces[k : k + 2]], axis=1)
            term = jnp.dot(pair, w_of(k, pair.shape[1]), preferred_element_type=jnp.float32)
            total = term if total is None else total + term
        return total

    def near_row(t, r):
        pieces = [lambda k=k: nears[t][near_idx[r, k]] for k in range(k_near)]
        total = chain(pieces, lambda k, n: weights[r, pl.ds(k * blk, n), :])
        acc[r] = total + drive[r].astype(jnp.float32)

    def blend(t, r, current, rates):
        leak = leak_ref[r]
        return ((1.0 - leak) * rates.astype(jnp.float32) + leak * jnp.tanh(current)).astype(
            jnp.bfloat16
        )

    def far_row(t, r, chunks):
        if len(chunks) == 1:
            rows_of = span(chunks[0])
        else:
            rows_of = slice(None)
        pieces = [
            lambda k=k: jnp.concatenate([fars[t][c][far_idx[r, k]] for c in chunks], axis=0)
            for k in range(k_far)
        ]
        total = chain(pieces, lambda k, n: weights[r, pl.ds((k_near + k) * blk, n), :])
        value = blend(t, r, acc[r, rows_of, :] + total, nears[t][r + 1, rows_of, :])
        if t + 1 < STEPS:
            nears[t + 1][r + 1, rows_of, :] = value
        else:
            out_ref[rows_of, pl.ds(pl.multiple_of(r * blk, blk), blk)] = value

    load(0).wait()
    for c in range(CHUNKS):
        send_export(0, c)
    send_low(0)
    load(rows - 1).wait()
    send_high(0)
    for r in range(1, rows - 1):
        load(r).wait()

    everything = list(range(CHUNKS))

    def near_rows(t, first, count):
        @pl.loop(first, first + count, unroll=UNROLL)
        def _(r):
            near_row(t, r)

    def near_part(t):
        wait_edges(t)
        share = rows // 2
        relay(t, 0)
        near_rows(t, 0, share)
        for c in range(1, 1 + LEAD):
            relay(t, c)
        near_rows(t, share, rows - share)

    for r in range(rows):
        load_weights(r).wait()
        load_drive(r).wait()
    near_part(0)
    for t in range(STEPS):
        last = t + 1 == STEPS
        for c in everything:
            wait_partner(t, c)
            if last:
                @pl.loop(0, rows, unroll=UNROLL)
                def _(r, t=t, c=c):
                    far_row(t, r, [c])
            if not last:
                far_row(t, 0, [c])
                send_export(t + 1, c)
            if c + 1 + LEAD < CHUNKS:
                relay(t, c + 1 + LEAD)
        if not last:
            send_low(t + 1)
            far_row(t, rows - 1, everything)
            send_high(t + 1)

            @pl.loop(1, rows - 1, unroll=rows - 2)
            def _(r, t=t):
                far_row(t, r, everything)

            near_part(t + 1)

    for t in range(STEPS):
        for c in everything:
            for offset in offsets(True):
                @pl.when(inside(offset))
                def _(t=t, c=c, offset=offset):
                    @pl.when(column_needs(member(offset), area))
                    def _():
                        column_copy(t, c, offset).wait_send()

                @pl.when(inside(offset))
                def _(t=t, c=c, offset=offset):
                    @pl.when(needs(partner, member(offset)))
                    def _():
                        relay_copy(t, c, offset).wait_send()

            @pl.when(needs(partner, area))
            def _(t=t, c=c):
                own_copy(t, c).wait_send()

        @pl.when(has_low)
        def _(t=t):
            low_copy(t).wait_send()

        @pl.when(has_high)
        def _(t=t):
            high_copy(t).wait_send()


def body(n_area, n_tile, start_rates, stim_drive, leak_rates, block_weights, near_index, far_index):
    _, batch, width = start_rates.shape
    _, rows, slots, blk, _ = block_weights.shape
    k_near, k_far = near_index.shape[-1], far_index.shape[-1]
    sizes = (n_area, n_tile, batch, rows, k_near, k_far, blk)
    n_col = n_area // 2
    part = batch // CHUNKS
    any_spec = pl.BlockSpec(memory_space=pl.ANY)
    smem_spec = pl.BlockSpec(memory_space=pltpu.SMEM)
    vmem_spec = pl.BlockSpec(memory_space=pltpu.VMEM)
    dma = pltpu.SemaphoreType.DMA
    scratch = (
        [pltpu.VMEM((rows + 2, batch, blk), jnp.bfloat16) for _ in range(STEPS)]
        + [pltpu.VMEM((n_area, part, blk), jnp.bfloat16) for _ in range(STEPS * CHUNKS)]
        + [
            pltpu.VMEM((rows, batch, blk), jnp.bfloat16),
            pltpu.VMEM((rows, slots * blk, blk), jnp.bfloat16),
            pltpu.VMEM((rows, batch, blk), jnp.float32),
            dma((rows,)),
            dma((rows,)),
            dma((rows,)),
            dma((STEPS, CHUNKS, n_area)),
            dma((STEPS, CHUNKS, 2 * n_col - 1)),
            dma((STEPS, CHUNKS)),
            dma((STEPS, CHUNKS, 2 * n_col - 1)),
            dma((STEPS, 2)),
            dma((STEPS, 2)),
        ]
    )
    out = pl.pallas_call(
        functools.partial(kernel, sizes),
        out_shape=pltpu.MemorySpace.VMEM((batch, width), jnp.bfloat16),
        in_specs=[smem_spec, smem_spec, any_spec, any_spec, vmem_spec, any_spec],
        out_specs=vmem_spec,
        scratch_shapes=scratch,
        compiler_params=pltpu.CompilerParams(
            collective_id=0, has_side_effects=True, vmem_limit_bytes=56 * 1024 * 1024
        ),
        name="rate_steps",
    )(
        near_index[0],
        far_index[0],
        start_rates[0],
        stim_drive[0],
        leak_rates[0].reshape(rows, 1, blk),
        block_weights[0].reshape(rows, slots * blk, blk),
    )
    return out[None]


def solution(mesh):
    in_specs = (
        P("area", None, "tile"),
        P("area", None, "tile"),
        P("area", "tile"),
        P("area", "tile", None, None, None),
        P("area", "tile", None),
        P("area", "tile", None),
    )
    out_specs = P("area", None, "tile")
    local = functools.partial(body, mesh.shape["area"], mesh.shape["tile"])
    return jax.shard_map(local, mesh=mesh, in_specs=in_specs, out_specs=out_specs, check_vma=False)
```

profile of v0, /device:TPU:0, one launch (start us, length us, event | category | flops | bytes accessed | tf_op | source)
XLA Modules:
  0.0 37.7 jit_solution(14275714432732184523)
XLA Ops:
  0.0 36.9 %rate_steps.1 = bf16[256,1024]{1,0:T(8,128)(2,1)S(1)} custom-call(s32[8,12]{1,0:T(8,128)} %bitcast.11, s32[8,8]{1,0:T(8,128)} %bitcast.12, bf16[256,1024]{1,0:T(8,128)(2,1)} %bitcast.9, bf16[256,1024]{1,0:T(8,128)(2,1)} %bitcast.10, f32[8,1,128]{2,1,0:T(1,128)} %bitcast.13, bf16[8,2560,128]{2,1,0:T(8,128)(2,1)} %bitcast.8), custom_call_target="tpu_custom_call" | custom-call | tf_op jit(solution)/shard_map/rate_steps/pallas_call | solution.py:380
  36.9 0.8 %copy.8 = bf16[1,256,1024]{2,1,0:T(8,128)(2,1)} copy(bf16[1,256,1024]{2,1,0:T(8,128)(2,1)S(1)} %bitcast.7) | data formatting | bytes 1048576
where the time goes:
time: 37.8 us; the launch traced here: 37.7 us
  Pallas kernels  36.9 us (98%)
  local copies, waits for them, and re-layouts  0.8 us (2%)
    pallas_call x1, Pallas kernels, body(): pl.pallas_call(functools.partial(kernel, sizes), out_shape=pltpu.MemorySp...  36.9 us
    unnamed x1, local copies, waits for them, and re-layouts  0.8 us

commit v1 on v0

v1 whole, which is shorter than its diff:
```python
import functools

import jax
import jax.numpy as jnp
from jax import lax
from jax.experimental import pallas as pl
from jax.experimental.pallas import tpu as pltpu
from jax.sharding import PartitionSpec as P

STEPS = 3
CHUNKS = 2
PIECES = 4
LONG = 3
ORDER = (
    ("down",),
    ("high",),
    ("fetch", 0),
    ("up", 1),
    ("across",),
    ("fetch", 1),
    ("up", 2),
    ("load",),
    ("relay", 0, 0, 1),
    ("relay", 0, 0, -1),
    ("start", 0),
    ("start", 1),
    ("relay", 0, 0, 2),
    ("relay", 0, 0, -2),
    ("relay", 0, 1, 1),
    ("relay", 0, 1, -1),
    ("up", 3),
    ("start", 2),
    ("start", 3),
    ("relay", 0, 0, 3),
    ("relay", 0, 0, -3),
    ("relay", 0, 1, 2),
    ("relay", 0, 1, -2),
    ("relay", 0, 1, 3),
    ("relay", 0, 1, -3),
    ("first", 0, 0),
    ("rest", 0, 0),
    ("first", 0, 1),
    ("rest", 0, 1),
    ("relay", 1, 0, 1),
    ("relay", 1, 0, -1),
    ("relay", 1, 0, 2),
    ("relay", 1, 0, -2),
    ("relay", 1, 0, 3),
    ("relay", 1, 0, -3),
    ("near", 1, 0),
    ("relay", 1, 1, 1),
    ("relay", 1, 1, -1),
    ("relay", 1, 1, 2),
    ("relay", 1, 1, -2),
    ("relay", 1, 1, 3),
    ("relay", 1, 1, -3),
    ("near", 1, 1),
    ("first", 1, 0),
    ("rest", 1, 0),
    ("first", 1, 1),
    ("rest", 1, 1),
    ("relay", 2, 0, 1),
    ("relay", 2, 0, -1),
    ("relay", 2, 0, 2),
    ("relay", 2, 0, -2),
    ("relay", 2, 0, 3),
    ("relay", 2, 0, -3),
    ("near", 2, 0),
    ("relay", 2, 1, 1),
    ("relay", 2, 1, -1),
    ("relay", 2, 1, 2),
    ("relay", 2, 1, -2),
    ("relay", 2, 1, 3),
    ("relay", 2, 1, -3),
    ("near", 2, 1),
    ("first", 2, 0),
    ("first", 2, 1),
)
FIRST = next(step[1] for step in ORDER if step[0] == "start")
MESH = pl.DeviceIdType.MESH


def group_of(section, n_area):
    unit = n_area // 8
    return (
        (section >= 3 * unit).astype(jnp.int32)
        + (section >= 5 * unit).astype(jnp.int32)
        + (section >= 7 * unit).astype(jnp.int32)
    )


def kernel(sizes, near_hbm, far_hbm, rates_hbm, drive_hbm, leak_hbm, w_hbm, out_ref, *scratch):
    n_area, n_tile = sizes[:2]
    n_col = n_area // 2
    dma = pltpu.SemaphoreType.DMA
    regular = pltpu.SemaphoreType.REGULAR
    refs = (near_hbm, far_hbm, rates_hbm, drive_hbm, leak_hbm, w_hbm, out_ref)
    pl.run_scoped(
        functools.partial(program, sizes, refs, scratch),
        dma((9,)),
        dma((2, CHUNKS, n_area)),
        dma((CHUNKS, 2 * n_col - 1)),
        dma((CHUNKS,)),
        dma((CHUNKS, 2 * n_col - 1)),
        dma((CHUNKS, 2)),
        dma((STEPS, CHUNKS, 2)),
        regular((n_col + 2,)),
    )


def program(
    sizes, refs, scratch,
    load_sem, far_recv, col_send, own_send, relay_send, edge_send, edge_recv, in_sem,
):
    n_area, n_tile, batch, rows, k_near, k_far, blk = sizes
    near_hbm, far_hbm, rates_hbm, drive_hbm, leak_hbm, w_hbm, out_ref = refs
    n_col = n_area // 2
    part = batch // CHUNKS
    chunks = range(CHUNKS)
    near_idx, far_idx, leak_ref, drive, weights, acc, start = scratch[:7]
    rest = scratch[7:]
    nears = {
        (t, c): rest[(t - 1) * CHUNKS + c] for t in range(1, STEPS) for c in chunks
    }
    rest = rest[(STEPS - 1) * CHUNKS :]
    fars = {(t, c): rest[t * CHUNKS + c] for t in range(STEPS) for c in chunks}

    area = lax.axis_index("area")
    tile = lax.axis_index("tile")
    side = lax.rem(area, 2)
    level = area // 2
    partner = area + 1 - 2 * side
    has_low = tile > 0
    has_high = tile < n_tile - 1

    def needs(section, source):
        return group_of(section, n_area) != group_of(source, n_area)

    def column_needs(section, source):
        mate = section + 1 - 2 * lax.rem(section, 2)
        return jnp.logical_or(needs(section, source), needs(mate, source))

    near_first = [s * d for d in range(1, n_col) for s in (1, -1)]
    far_first = [s * d for d in range(n_col - 1, 0, -1) for s in (1, -1)]

    def inside(offset):
        return jnp.logical_and(level + offset >= 0, level + offset < n_col)

    def member(offset):
        return area + 2 * offset

    def span(c):
        return pl.ds(c * part, part)

    barrier = pltpu.get_barrier_semaphore()
    in_x, in_t = 0, n_col + 1

    for d in range(1, n_col):
        @pl.when(inside(d))
        def _(d=d):
            pl.semaphore_signal(barrier, inc=1, device_id=(member(d), tile), device_id_type=MESH)

    @pl.when(side == 0)
    def _():
        pl.semaphore_signal(barrier, inc=1, device_id=(partner, tile), device_id_type=MESH)

    @pl.when(has_high)
    def _():
        pl.semaphore_signal(barrier, inc=1, device_id=(area, tile + 1), device_id_type=MESH)

    def load(r, sem):
        return pltpu.make_async_copy(
            rates_hbm.at[:, pl.ds(r * blk, blk)], start.at[r + 1], load_sem.at[sem]
        )

    def load_drive(r):
        return pltpu.make_async_copy(
            drive_hbm.at[:, pl.ds(r * blk, blk)], drive.at[r], load_sem.at[2]
        )

    near_part, far_part = pl.ds(0, k_near * blk), pl.ds(k_near * blk, k_far * blk)

    def load_near_weights(r):
        return pltpu.make_async_copy(
            w_hbm.at[r, near_part], weights.at[r, near_part], load_sem.at[1]
        )

    def load_far_weights(r):
        return pltpu.make_async_copy(
            w_hbm.at[r, far_part], weights.at[r, far_part], load_sem.at[8]
        )

    load_near = pltpu.make_async_copy(near_hbm, near_idx, load_sem.at[3])
    load_far = pltpu.make_async_copy(far_hbm, far_idx, load_sem.at[4])
    load_leak = pltpu.make_async_copy(leak_hbm, leak_ref, load_sem.at[5])

    load(0, 6).start()
    load(rows - 1, 7).start()
    load_near.start()
    load_far.start()
    load_leak.start()

    def fetch(part_of):
        if part_of == 0:
            for r in range(1, rows - 1):
                load(r, 0).start()
            for r in range(rows):
                load_near_weights(r).start()
                load_drive(r).start()
        else:
            for r in range(rows):
                load_far_weights(r).start()

    below = level + side + has_low.astype(jnp.int32)

    @pl.when(below > 0)
    def _():
        pl.semaphore_wait(barrier, below)

    for d in range(1, n_col):
        @pl.when(inside(-d))
        def _(d=d):
            pl.semaphore_signal(
                in_sem.at[d], inc=1, device_id=(member(-d), tile), device_id_type=MESH
            )

    @pl.when(side == 1)
    def _():
        pl.semaphore_signal(in_sem.at[in_x], inc=1, device_id=(partner, tile), device_id_type=MESH)

    @pl.when(has_low)
    def _():
        pl.semaphore_signal(
            in_sem.at[in_t], inc=1, device_id=(area, tile - 1), device_id_type=MESH
        )

    def block_of(t, c, r):
        return start.at[r + 1, span(c)] if t == 0 else nears[t, c].at[r + 1]

    def column_copy(t, c, offset):
        return pltpu.make_async_remote_copy(
            src_ref=block_of(t, c, 0),
            dst_ref=fars[t, c].at[area],
            send_sem=col_send.at[c, offset + n_col - 1],
            recv_sem=far_recv.at[t % 2, c, area],
            device_id=(member(offset), tile),
            device_id_type=MESH,
        )

    def own_copy(t, c):
        return pltpu.make_async_remote_copy(
            src_ref=block_of(t, c, 0),
            dst_ref=fars[t, c].at[area],
            send_sem=own_send.at[c],
            recv_sem=far_recv.at[t % 2, c, area],
            device_id=(partner, tile),
            device_id_type=MESH,
        )

    def relay_copy(t, c, offset):
        source = member(offset)
        return pltpu.make_async_remote_copy(
            src_ref=fars[t, c].at[source],
            dst_ref=fars[t, c].at[source],
            send_sem=relay_send.at[c, offset + n_col - 1],
            recv_sem=far_recv.at[t % 2, c, source],
            device_id=(partner, tile),
            device_id_type=MESH,
        )

    def arrival(t, c, source):
        return pltpu.make_async_remote_copy(
            src_ref=block_of(t, c, 0),
            dst_ref=fars[t, c].at[source],
            send_sem=own_send.at[c],
            recv_sem=far_recv.at[t % 2, c, source],
            device_id=(partner, tile),
            device_id_type=MESH,
        )

    def low_copy(t, c):
        return pltpu.make_async_remote_copy(
            src_ref=start.at[1] if t == 0 else nears[t, c].at[1],
            dst_ref=start.at[rows + 1] if t == 0 else nears[t, c].at[rows + 1],
            send_sem=edge_send.at[c, 0],
            recv_sem=edge_recv.at[t, c, 1],
            device_id=(area, tile - 1),
            device_id_type=MESH,
        )

    def high_copy(t, c):
        return pltpu.make_async_remote_copy(
            src_ref=start.at[rows] if t == 0 else nears[t, c].at[rows],
            dst_ref=start.at[0] if t == 0 else nears[t, c].at[0],
            send_sem=edge_send.at[c, 1],
            recv_sem=edge_recv.at[t, c, 0],
            device_id=(area, tile + 1),
            device_id_type=MESH,
        )

    def column_step(t, c, offset, act):
        @pl.when(inside(offset))
        def _():
            @pl.when(column_needs(member(offset), area))
            def _():
                act(column_copy(t, c, offset))

    def own_step(t, c, act):
        @pl.when(needs(partner, area))
        def _():
            act(own_copy(t, c))

    def relay_step(t, c, offset, act):
        @pl.when(inside(offset))
        def _():
            @pl.when(needs(partner, member(offset)))
            def _():
                act(relay_copy(t, c, offset))

    def edge_step(t, c, low, act):
        @pl.when(has_low if low else has_high)
        def _():
            act((low_copy if low else high_copy)(t, c))

    def go(copy):
        copy.start()

    def sent(copy):
        copy.wait_send()

    def export_sent(t, c):
        for offset in far_first:
            column_step(t, c, offset, sent)
        own_step(t, c, sent)

    def send_export(t, c):
        for offset in far_first:
            column_step(t, c, offset, go)
        own_step(t, c, go)

    def edges_sent(t, c):
        edge_step(t, c, True, sent)
        edge_step(t, c, False, sent)

    def wait_edges(t, c):
        @pl.when(has_high)
        def _():
            low_copy(t, c).wait_recv()

        @pl.when(has_low)
        def _():
            high_copy(t, c).wait_recv()

    def relay(t, c, offset):
        @pl.when(inside(offset))
        def _():
            @pl.when(needs(partner, member(offset)))
            def _():
                arrival(t, c, member(offset)).wait_recv()
                if t > 0:
                    relay_copy(t - 1, c, offset).wait_send()
                relay_copy(t, c, offset).start()

    def wait_far(t, c):
        @pl.when(needs(area, partner))
        def _():
            arrival(t, c, partner).wait_recv()

        for offset in near_first:
            @pl.when(inside(offset))
            def _(offset=offset):
                column, across = member(offset), partner + 2 * offset
                direct = jnp.logical_not(needs(partner, column))

                @pl.when(jnp.logical_and(direct, needs(area, column)))
                def _():
                    arrival(t, c, column).wait_recv()

                @pl.when(needs(area, across))
                def _():
                    arrival(t, c, across).wait_recv()

    def chain(pieces, w_of):
        total = None
        for k in range(0, len(pieces), 2):
            pair = jnp.concatenate([p() for p in pieces[k : k + 2]], axis=1)
            term = jnp.dot(pair, w_of(k, pair.shape[1]), preferred_element_type=jnp.float32)
            total = term if total is None else total + term
        return total

    def near_row(buffer, r, rows_of):
        pieces = [lambda k=k: buffer[near_idx[r, k]] for k in range(k_near)]
        total = chain(pieces, lambda k, n: weights[r, pl.ds(k * blk, n), :])
        acc[r, rows_of, :] = total + drive[r, rows_of, :].astype(jnp.float32)

    def far_row(t, c, r):
        pieces = [lambda k=k: fars[t, c][far_idx[r, k]] for k in range(k_far)]
        total = chain(pieces, lambda k, n: weights[r, pl.ds((k_near + k) * blk, n), :])
        current = acc[r, span(c), :] + total
        rates = start[r + 1, span(c), :] if t == 0 else nears[t, c][r + 1]
        leak = leak_ref[r]
        value = ((1.0 - leak) * rates.astype(jnp.float32) + leak * jnp.tanh(current)).astype(
            jnp.bfloat16
        )
        if t + 1 < STEPS:
            nears[t + 1, c][r + 1] = value
        else:
            out_ref[span(c), pl.ds(pl.multiple_of(r * blk, blk), blk)] = value

    def near_start(piece):
        count = rows // PIECES
        if piece == FIRST:
            wait_edges(0, 0)

        @pl.loop(piece * count, (piece + 1) * count, unroll=count)
        def _(r):
            near_row(start, r, slice(None))

    def near_chunk(t, c):
        wait_edges(t, c)

        @pl.loop(0, rows, unroll=rows // 2)
        def _(r):
            near_row(nears[t, c], r, span(c))

    def far_first_row(t, c):
        if (t, c) == (0, 0):
            load_last()
        wait_far(t, c)
        if t + 1 == STEPS:
            @pl.loop(0, rows, unroll=rows // 2)
            def _(r):
                far_row(t, c, r)

            return
        export_sent(t, c)
        far_row(t, c, 0)
        send_export(t + 1, c)

    def far_rest(t, c):
        if t > 0 or c == 0:
            edges_sent(t, c)
        edge_step(t + 1, c, True, go)

        @pl.loop(1, rows, unroll=rows - 1)
        def _(r):
            far_row(t, c, r)

        edge_step(t + 1, c, False, go)

    def send_down():
        load(0, 6).wait()
        for c in chunks:
            for d in range(n_col - 1, 0, -1):
                column_step(0, c, -d, go)

        @pl.when(side == 1)
        def _():
            for c in chunks:
                own_step(0, c, go)

        edge_step(0, 0, True, go)

    def send_high():
        load(rows - 1, 7).wait()

        @pl.when(has_high)
        def _():
            pl.semaphore_wait(in_sem.at[in_t], 1)

        edge_step(0, 0, False, go)

    def send_across():
        @pl.when(side == 0)
        def _():
            pl.semaphore_wait(in_sem.at[in_x], 1)
            for c in chunks:
                own_step(0, c, go)

    def send_up(d):
        @pl.when(inside(d))
        def _():
            pl.semaphore_wait(in_sem.at[d], 1)

        for c in chunks:
            column_step(0, c, d, go)

    def load_rest():
        zeros = jnp.zeros((part, blk), jnp.bfloat16)

        @pl.when(jnp.logical_not(has_low))
        def _():
            start[0] = jnp.zeros((batch, blk), jnp.bfloat16)
            for key in nears:
                nears[key][0] = zeros

        @pl.when(jnp.logical_not(has_high))
        def _():
            start[rows + 1] = jnp.zeros((batch, blk), jnp.bfloat16)
            for key in nears:
                nears[key][rows + 1] = zeros

        inner = start.at[pl.ds(2, rows - 2)]
        pltpu.make_async_copy(inner, inner, load_sem.at[0]).wait()
        load_near.wait()
        near_weights = weights.at[:, near_part]
        pltpu.make_async_copy(near_weights, near_weights, load_sem.at[1]).wait()
        pltpu.make_async_copy(drive, drive, load_sem.at[2]).wait()

    def load_last():
        far_weights = weights.at[:, far_part]
        pltpu.make_async_copy(far_weights, far_weights, load_sem.at[8]).wait()
        load_far.wait()
        load_leak.wait()

    steps = {
        "down": send_down,
        "across": send_across,
        "high": send_high,
        "up": send_up,
        "load": load_rest,
        "fetch": fetch,
        "start": near_start,
        "first": far_first_row,
        "rest": far_rest,
        "near": near_chunk,
    }
    for name, *at in ORDER:
        if name == "up" and at[0] >= LONG:
            for d in range(LONG, n_col):
                send_up(d)
        elif name == "up":
            if at[0] < n_col:
                send_up(*at)
        elif name == "relay":
            t, c, offset = at
            away = abs(offset)
            if away >= LONG:
                for d in range(LONG, n_col):
                    relay(t, c, d if offset > 0 else -d)
            elif away < n_col:
                relay(t, c, offset)
        else:
            steps[name](*at)

    t = STEPS - 1
    for c in chunks:
        export_sent(t, c)
        for offset in near_first:
            relay_step(t, c, offset, sent)
        edges_sent(t, c)


def body(n_area, n_tile, start_rates, stim_drive, leak_rates, block_weights, near_index, far_index):
    _, batch, width = start_rates.shape
    _, rows, slots, blk, _ = block_weights.shape
    k_near, k_far = near_index.shape[-1], far_index.shape[-1]
    sizes = (n_area, n_tile, batch, rows, k_near, k_far, blk)
    part = batch // CHUNKS
    any_spec = pl.BlockSpec(memory_space=pl.ANY)
    vmem_spec = pl.BlockSpec(memory_space=pltpu.VMEM)
    scratch = (
        [
            pltpu.SMEM((rows, k_near), jnp.int32),
            pltpu.SMEM((rows, k_far), jnp.int32),
            pltpu.VMEM((rows, 1, blk), jnp.float32),
            pltpu.VMEM((rows, batch, blk), jnp.bfloat16),
            pltpu.VMEM((rows, slots * blk, blk), jnp.bfloat16),
            pltpu.VMEM((rows, batch, blk), jnp.float32),
            pltpu.VMEM((rows + 2, batch, blk), jnp.bfloat16),
        ]
        + [pltpu.VMEM((rows + 2, part, blk), jnp.bfloat16) for _ in range((STEPS - 1) * CHUNKS)]
        + [pltpu.VMEM((n_area, part, blk), jnp.bfloat16) for _ in range(STEPS * CHUNKS)]
    )
    out = pl.pallas_call(
        functools.partial(kernel, sizes),
        out_shape=pltpu.MemorySpace.VMEM((batch, width), jnp.bfloat16),
        in_specs=[any_spec] * 6,
        out_specs=vmem_spec,
        scratch_shapes=scratch,
        compiler_params=pltpu.CompilerParams(
            collective_id=0, has_side_effects=True, vmem_limit_bytes=56 * 1024 * 1024
        ),
        name="rate_steps",
    )(
        near_index[0],
        far_index[0],
        start_rates[0],
        stim_drive[0],
        leak_rates[0].reshape(rows, 1, blk),
        block_weights[0].reshape(rows, slots * blk, blk),
    )
    return out[None]


def solution(mesh):
    in_specs = (
        P("area", None, "tile"),
        P("area", None, "tile"),
        P("area", "tile"),
        P("area", "tile", None, None, None),
        P("area", "tile", None),
        P("area", "tile", None),
    )
    out_specs = P("area", None, "tile")
    local = functools.partial(body, mesh.shape["area"], mesh.shape["tile"])
    return jax.shard_map(local, mesh=mesh, in_specs=in_specs, out_specs=out_specs, check_vma=False)
```

time: 37.8 us -> 35 us (0.926)
  Pallas kernels: 36.9 us -> 34 us
    pallas_call x1, Pallas kernels: 36.9 us -> 34 us  [body(): pl.pallas_call(functools.partial(kernel, sizes), out_shape=pltpu.MemorySp...]
where the time goes in v1:
time: 35 us; the launch traced here: 34.8 us
  Pallas kernels  34 us (97%)
  local copies, waits for them, and re-layouts  0.8 us (2%)
    pallas_call x1, Pallas kernels, body(): pl.pallas_call(functools.partial(kernel, sizes), out_shape=pltpu.MemorySp...  34 us
    unnamed x1, local copies, waits for them, and re-layouts  0.8 us

profile of v1, /device:TPU:0, one launch (start us, length us, event | category | flops | bytes accessed | tf_op | source)
XLA Modules:
  0.0 34.8 jit_solution(16928999332141194987)
XLA Ops:
  0.0 34.0 %rate_steps.1 = bf16[256,1024]{1,0:T(8,128)(2,1)S(1)} custom-call(s32[8,12]{1,0:T(8,128)} %bitcast.11, s32[8,8]{1,0:T(8,128)} %bitcast.12, bf16[256,1024]{1,0:T(8,128)(2,1)} %bitcast.9, bf16[256,1024]{1,0:T(8,128)(2,1)} %bitcast.10, f32[8,1,128]{2,1,0:T(1,128)} %bitcast.13, bf16[8,2560,128]{2,1,0:T(8,128)(2,1)} %bitcast.8), custom_call_target="tpu_custom_call" | custom-call | tf_op jit(solution)/shard_map/rate_steps/pallas_call | solution.py:575
  34.1 0.8 %copy.8 = bf16[1,256,1024]{2,1,0:T(8,128)(2,1)} copy(bf16[1,256,1024]{2,1,0:T(8,128)(2,1)S(1)} %bitcast.7) | data formatting | bytes 1048576

commit v2 on v1

--- a/solution.py
+++ b/solution.py
@@ -12,69 +12,20 @@
 PIECES = 4
 LONG = 3
 ORDER = (
-    ("down",),
-    ("high",),
-    ("fetch", 0),
-    ("up", 1),
-    ("across",),
-    ("fetch", 1),
-    ("up", 2),
-    ("load",),
-    ("relay", 0, 0, 1),
-    ("relay", 0, 0, -1),
-    ("start", 0),
-    ("start", 1),
-    ("relay", 0, 0, 2),
-    ("relay", 0, 0, -2),
-    ("relay", 0, 1, 1),
-    ("relay", 0, 1, -1),
-    ("up", 3),
-    ("start", 2),
-    ("start", 3),
-    ("relay", 0, 0, 3),
-    ("relay", 0, 0, -3),
-    ("relay", 0, 1, 2),
-    ("relay", 0, 1, -2),
-    ("relay", 0, 1, 3),
-    ("relay", 0, 1, -3),
-    ("first", 0, 0),
-    ("rest", 0, 0),
-    ("first", 0, 1),
-    ("rest", 0, 1),
-    ("relay", 1, 0, 1),
-    ("relay", 1, 0, -1),
-    ("relay", 1, 0, 2),
-    ("relay", 1, 0, -2),
-    ("relay", 1, 0, 3),
-    ("relay", 1, 0, -3),
-    ("near", 1, 0),
-    ("relay", 1, 1, 1),
-    ("relay", 1, 1, -1),
-    ("relay", 1, 1, 2),
-    ("relay", 1, 1, -2),
-    ("relay", 1, 1, 3),
-    ("relay", 1, 1, -3),
-    ("near", 1, 1),
-    ("first", 1, 0),
-    ("rest", 1, 0),
-    ("first", 1, 1),
-    ("rest", 1, 1),
-    ("relay", 2, 0, 1),
-    ("relay", 2, 0, -1),
-    ("relay", 2, 0, 2),
-    ("relay", 2, 0, -2),
-    ("relay", 2, 0, 3),
-    ("relay", 2, 0, -3),
-    ("near", 2, 0),
-    ("relay", 2, 1, 1),
-    ("relay", 2, 1, -1),
-    ("relay", 2, 1, 2),
-    ("relay", 2, 1, -2),
-    ("relay", 2, 1, 3),
-    ("relay", 2, 1, -3),
-    ("near", 2, 1),
-    ("first", 2, 0),
-    ("first", 2, 1),
+    ("down",), ("high",), ("fetch", 0), ("up", 1), ("across",), ("fetch", 1), ("up", 2),
+    ("load",), ("start", 0), ("start", 1), ("up", 3), ("start", 2), ("late", 1),
+    ("relay", 0, 0, 1), ("relay", 0, 0, -1), ("relay", 0, 0, 2), ("relay", 0, 0, -2),
+    ("start", 3), ("relay", 0, 0, 3), ("relay", 0, 0, -3), ("relay", 0, 1, 1),
+    ("relay", 0, 1, -1), ("relay", 0, 1, 2), ("relay", 0, 1, -2), ("relay", 0, 1, 3),
+    ("relay", 0, 1, -3), ("first", 0, 0), ("rest", 0, 0), ("first", 0, 1), ("rest", 0, 1),
+    ("relay", 1, 0, 1), ("relay", 1, 0, -1), ("relay", 1, 0, 2), ("relay", 1, 0, -2),
+    ("relay", 1, 0, 3), ("relay", 1, 0, -3), ("near", 1, 0), ("relay", 1, 1, 1),
+    ("relay", 1, 1, -1), ("relay", 1, 1, 2), ("relay", 1, 1, -2), ("relay", 1, 1, 3),
+    ("relay", 1, 1, -3), ("first", 1, 0), ("rest", 1, 0), ("near", 1, 1), ("first", 1, 1),
+    ("rest", 1, 1), ("relay", 2, 0, 1), ("relay", 2, 0, -1), ("relay", 2, 0, 2),
+    ("relay", 2, 0, -2), ("relay", 2, 0, 3), ("relay", 2, 0, -3), ("near", 2, 0),
+    ("relay", 2, 1, 1), ("relay", 2, 1, -1), ("relay", 2, 1, 2), ("relay", 2, 1, -2),
+    ("relay", 2, 1, 3), ("relay", 2, 1, -3), ("first", 2, 0), ("near", 2, 1), ("first", 2, 1),
 )
 FIRST = next(step[1] for step in ORDER if step[0] == "start")
 MESH = pl.DeviceIdType.MESH
@@ -450,14 +401,12 @@
 
     def send_down():
         load(0, 6).wait()
-        for c in chunks:
-            for d in range(n_col - 1, 0, -1):
-                column_step(0, c, -d, go)
+        for d in range(n_col - 1, 0, -1):
+            column_step(0, 0, -d, go)
 
         @pl.when(side == 1)
         def _():
-            for c in chunks:
-                own_step(0, c, go)
+            own_step(0, 0, go)
 
         edge_step(0, 0, True, go)
 
@@ -474,16 +423,19 @@
         @pl.when(side == 0)
         def _():
             pl.semaphore_wait(in_sem.at[in_x], 1)
-            for c in chunks:
-                own_step(0, c, go)
+            own_step(0, 0, go)
 
     def send_up(d):
         @pl.when(inside(d))
         def _():
             pl.semaphore_wait(in_sem.at[d], 1)
 
-        for c in chunks:
-            column_step(0, c, d, go)
+        column_step(0, 0, d, go)
+
+    def send_late(c):
+        for offset in far_first:
+            column_step(0, c, offset, go)
+        own_step(0, c, go)
 
     def load_rest():
         zeros = jnp.zeros((part, blk), jnp.bfloat16)
@@ -520,6 +472,7 @@
         "up": send_up,
         "load": load_rest,
         "fetch": fetch,
+        "late": send_late,
         "start": near_start,
         "first": far_first_row,
         "rest": far_rest,

time: 35 us -> 33.5 us (0.957)
  Pallas kernels: 34 us -> 32.5 us
    pallas_call x1, Pallas kernels: 34 us -> 32.5 us  [body(): pl.pallas_call(functools.partial(kernel, sizes), out_shape=pltpu.MemorySp...]
where the time goes in v2:
time: 33.5 us; the launch traced here: 33.3 us
  Pallas kernels  32.5 us (97%)
  local copies, waits for them, and re-layouts  0.8 us (2%)
    pallas_call x1, Pallas kernels, body(): pl.pallas_call(functools.partial(kernel, sizes), out_shape=pltpu.MemorySp...  32.5 us
    unnamed x1, local copies, waits for them, and re-layouts  0.8 us

profile of v2, /device:TPU:0, one launch (start us, length us, event | category | flops | bytes accessed | tf_op | source)
XLA Modules:
  0.0 33.3 jit_solution(13677511405340328056)
XLA Ops:
  0.0 32.5 %rate_steps.1 = bf16[256,1024]{1,0:T(8,128)(2,1)S(1)} custom-call(s32[8,12]{1,0:T(8,128)} %bitcast.11, s32[8,8]{1,0:T(8,128)} %bitcast.12, bf16[256,1024]{1,0:T(8,128)(2,1)} %bitcast.9, bf16[256,1024]{1,0:T(8,128)(2,1)} %bitcast.10, f32[8,1,128]{2,1,0:T(1,128)} %bitcast.13, bf16[8,2560,128]{2,1,0:T(8,128)(2,1)} %bitcast.8), custom_call_target="tpu_custom_call" | custom-call | tf_op jit(solution)/shard_map/rate_steps/pallas_call | solution.py:528
  32.5 0.8 %copy.8 = bf16[1,256,1024]{2,1,0:T(8,128)(2,1)} copy(bf16[1,256,1024]{2,1,0:T(8,128)(2,1)S(1)} %bitcast.7) | data formatting | bytes 1048576

commit v3 on v2

--- a/solution.py
+++ b/solution.py
@@ -13,19 +13,19 @@
 LONG = 3
 ORDER = (
     ("down",), ("high",), ("fetch", 0), ("up", 1), ("across",), ("fetch", 1), ("up", 2),
-    ("load",), ("start", 0), ("start", 1), ("up", 3), ("start", 2), ("late", 1),
+    ("load",), ("start", 0), ("up", 3), ("late", 1), ("start", 1), ("start", 2),
     ("relay", 0, 0, 1), ("relay", 0, 0, -1), ("relay", 0, 0, 2), ("relay", 0, 0, -2),
     ("start", 3), ("relay", 0, 0, 3), ("relay", 0, 0, -3), ("relay", 0, 1, 1),
     ("relay", 0, 1, -1), ("relay", 0, 1, 2), ("relay", 0, 1, -2), ("relay", 0, 1, 3),
-    ("relay", 0, 1, -3), ("first", 0, 0), ("rest", 0, 0), ("first", 0, 1), ("rest", 0, 1),
-    ("relay", 1, 0, 1), ("relay", 1, 0, -1), ("relay", 1, 0, 2), ("relay", 1, 0, -2),
+    ("relay", 0, 1, -3), ("first", 0, 0), ("rest", 0, 0), ("first", 0, 1), ("relay", 1, 0, 1),
+    ("relay", 1, 0, -1), ("rest", 0, 1), ("relay", 1, 0, 2), ("relay", 1, 0, -2),
     ("relay", 1, 0, 3), ("relay", 1, 0, -3), ("near", 1, 0), ("relay", 1, 1, 1),
     ("relay", 1, 1, -1), ("relay", 1, 1, 2), ("relay", 1, 1, -2), ("relay", 1, 1, 3),
     ("relay", 1, 1, -3), ("first", 1, 0), ("rest", 1, 0), ("near", 1, 1), ("first", 1, 1),
-    ("rest", 1, 1), ("relay", 2, 0, 1), ("relay", 2, 0, -1), ("relay", 2, 0, 2),
+    ("relay", 2, 0, 1), ("relay", 2, 0, -1), ("rest", 1, 1), ("relay", 2, 0, 2),
     ("relay", 2, 0, -2), ("relay", 2, 0, 3), ("relay", 2, 0, -3), ("near", 2, 0),
     ("relay", 2, 1, 1), ("relay", 2, 1, -1), ("relay", 2, 1, 2), ("relay", 2, 1, -2),
-    ("relay", 2, 1, 3), ("relay", 2, 1, -3), ("first", 2, 0), ("near", 2, 1), ("first", 2, 1),
+    ("relay", 2, 1, 3), ("relay", 2, 1, -3), ("near", 2, 1), ("first", 2, 0), ("first", 2, 1),
 )
 FIRST = next(step[1] for step in ORDER if step[0] == "start")
 MESH = pl.DeviceIdType.MESH
@@ -285,9 +285,9 @@
         own_step(t, c, sent)
 
     def send_export(t, c):
+        own_step(t, c, go)
         for offset in far_first:
             column_step(t, c, offset, go)
-        own_step(t, c, go)
 
     def edges_sent(t, c):
         edge_step(t, c, True, sent)
@@ -370,7 +370,7 @@
     def near_chunk(t, c):
         wait_edges(t, c)
 
-        @pl.loop(0, rows, unroll=rows // 2)
+        @pl.loop(0, rows, unroll=rows)
         def _(r):
             near_row(nears[t, c], r, span(c))
 
@@ -379,7 +379,7 @@
             load_last()
         wait_far(t, c)
         if t + 1 == STEPS:
-            @pl.loop(0, rows, unroll=rows // 2)
+            @pl.loop(0, rows, unroll=rows)
             def _(r):
                 far_row(t, c, r)
 
@@ -406,7 +406,8 @@
 
         @pl.when(side == 1)
         def _():
-            own_step(0, 0, go)
+            for c in chunks:
+                own_step(0, c, go)
 
         edge_step(0, 0, True, go)
 
@@ -423,7 +424,8 @@
         @pl.when(side == 0)
         def _():
             pl.semaphore_wait(in_sem.at[in_x], 1)
-            own_step(0, 0, go)
+            for c in chunks:
+                own_step(0, c, go)
 
     def send_up(d):
         @pl.when(inside(d))
@@ -435,7 +437,6 @@
     def send_late(c):
         for offset in far_first:
             column_step(0, c, offset, go)
-        own_step(0, c, go)
 
     def load_rest():
         zeros = jnp.zeros((part, blk), jnp.bfloat16)

time: 33.5 us -> 32.7 us (0.976)
  Pallas kernels: 32.5 us -> 31.7 us
    pallas_call x1, Pallas kernels: 32.5 us -> 31.7 us  [body(): pl.pallas_call(functools.partial(kernel, sizes), out_shape=pltpu.MemorySp...]
where the time goes in v3:
time: 32.7 us; the launch traced here: 32.6 us
  Pallas kernels  31.7 us (97%)
  local copies, waits for them, and re-layouts  0.8 us (2%)
    pallas_call x1, Pallas kernels, body(): pl.pallas_call(functools.partial(kernel, sizes), out_shape=pltpu.MemorySp...  31.7 us
    unnamed x1, local copies, waits for them, and re-layouts  0.8 us

profile of v3, /device:TPU:0, one launch (start us, length us, event | category | flops | bytes accessed | tf_op | source)
XLA Modules:
  0.0 32.6 jit_solution(17027000562775790729)
XLA Ops:
  0.0 31.7 %rate_steps.1 = bf16[256,1024]{1,0:T(8,128)(2,1)S(1)} custom-call(s32[8,12]{1,0:T(8,128)} %bitcast.11, s32[8,8]{1,0:T(8,128)} %bitcast.12, bf16[256,1024]{1,0:T(8,128)(2,1)} %bitcast.9, bf16[256,1024]{1,0:T(8,128)(2,1)} %bitcast.10, f32[8,1,128]{2,1,0:T(1,128)} %bitcast.13, bf16[8,2560,128]{2,1,0:T(8,128)(2,1)} %bitcast.8), custom_call_target="tpu_custom_call" | custom-call | tf_op jit(solution)/shard_map/rate_steps/pallas_call | solution.py:529
  31.8 0.8 %copy.8 = bf16[1,256,1024]{2,1,0:T(8,128)(2,1)} copy(bf16[1,256,1024]{2,1,0:T(8,128)(2,1)S(1)} %bitcast.7) | data formatting | bytes 1048576
